TPU v7x, 128 devices: a whole 4x4x4 slice. The times are simulated.
128 devices in a mesh: clu: 32 (over y, z, core), sub: 4 (over x).
Axes of the slice: x: 4, y: 4, z: 4, core: 2. Of those that a mesh axis runs over, the one named last changes fastest.
Arguments:
- points: bfloat16 [1024, 1024, 128], P('clu', 'sub'), may hold values from -6 to 6
- row_sketch: bfloat16 [32, 32, 1024, 128], P('clu', 'sub'), may hold values from -0.75 to 0.75
- col_sketch: bfloat16 [32, 32, 1024, 128], P('clu', 'sub'), may hold values from -0.75 to 0.75
- pair_count: int32 [32], P('clu'), may hold values from 4 to 32
- pair_local: int32 [32, 32], P('clu'), may hold values from 0 to 31
- pair_src: int32 [32, 32], P('clu'), may hold values from 0 to 31, as said below
- pair_partner: int32 [32, 32], P('clu'), may hold values from 0 to 31
- pair_rank: int32 [32, 32], P('clu'), may hold values from 64 to 128
Outputs:
- row_factor: bfloat16 [32, 32, 1024, 128], P('clu', 'sub')
- col_factor: bfloat16 [32, 32, 2, 1024, 128], P('clu', None, None, 'sub')
Inputs may be any that keep to these rules, and one draw needn't show every extreme that they name: `pair_src`: in each group's row every source group appears exactly 2 times or not at all, and its 2 slots p lie in 2 different blocks p // 8.
All inputs are finite; a program needn't handle non-finite values.
Results may differ from a plain program's by a relative error of at most 0.0049.
Values may be sent and summed in bfloat16 or wider, within the bound.
A program may use at most 128 MiB of HBM per device.

v0:
```python
import jax
import jax.numpy as jnp
from jax import lax
from jax.sharding import PartitionSpec as P

CAP = 2


def in_one_piece(arrays, axis, split_dim, concat_dim, along):
    widths = [a.shape[along] for a in arrays]
    both = jnp.concatenate(arrays, axis=along)
    filled = lax.all_to_all(both, axis, split_axis=split_dim, concat_axis=concat_dim, tiled=True)
    return tuple(jnp.split(filled, [sum(widths[:k]) for k in range(1, len(widths))], axis=along))


def kernel_tile(left_points, right_points):
    left_norm = jnp.sum(jnp.square(left_points.astype(jnp.float32)), axis=1)
    right_norm = jnp.sum(jnp.square(right_points.astype(jnp.float32)), axis=1)
    inner_term = jnp.dot(left_points, right_points.T, preferred_element_type=jnp.float32)
    return jnp.exp(
        -(left_norm[:, None] + right_norm[None, :] - 2.0 * inner_term) / right_points.shape[1]
    )


def slot_numbers(sources):
    position = jnp.arange(sources.shape[0], dtype=jnp.int32)
    earlier_same = (sources[:, None] == sources[None, :]) & (position[None, :] < position[:, None])
    return jnp.sum(earlier_same.astype(jnp.int32), axis=1)


def select_rows(choose_index, row_table):
    table_rows = row_table.shape[0]
    picked = (choose_index[:, None] == jnp.arange(table_rows, dtype=jnp.int32)[None, :]).astype(
        jnp.bfloat16
    )
    return jnp.dot(picked, row_table, preferred_element_type=jnp.float32).astype(jnp.bfloat16)


def shards(
    points, row_sketch, col_sketch, pair_count, pair_local, pair_src, pair_partner, pair_rank
):
    group_count = lax.axis_size("clu")
    sub_count = lax.axis_size("sub")
    my_sub = lax.axis_index("sub")
    clusters, strip_rows, feature_dim = points.shape
    pair_slots = pair_src.shape[1]
    own_pairs = pair_slots // sub_count
    sketch_rank = row_sketch.shape[3]
    length = strip_rows * sub_count
    first_pair = my_sub * own_pairs
    sources = pair_src[0]
    target = sources * CAP + slot_numbers(sources)
    slot_hits = target[:, None] == jnp.arange(group_count * CAP, dtype=jnp.int32)[None, :]
    owners = jnp.arange(pair_slots, dtype=jnp.int32) // own_pairs
    wanted = jnp.sum(jnp.where(slot_hits, pair_partner[0][:, None] + 1, 0), axis=0) - 1
    wanted_owner = jnp.sum(jnp.where(slot_hits, owners[:, None] + 1, 0), axis=0) - 1
    asked_for, asked_owner = in_one_piece(
        (wanted.reshape(group_count, CAP), wanted_owner.reshape(group_count, CAP)), "clu", 0, 0, 1
    )
    flat_points = points.reshape(clusters, strip_rows * feature_dim)
    outgoing = select_rows(asked_for.reshape(-1), flat_points)
    owner_strips = select_rows(pair_local[0], flat_points)
    arrived = lax.all_to_all(
        outgoing.reshape(group_count, CAP * strip_rows * feature_dim),
        "clu",
        split_axis=0,
        concat_axis=0,
        tiled=True,
    )
    partner_strips = jnp.dot(
        slot_hits.astype(jnp.bfloat16),
        arrived.reshape(group_count * CAP, strip_rows * feature_dim),
        preferred_element_type=jnp.float32,
    ).astype(jnp.bfloat16)
    left_rows, right_rows = (
        lax.all_to_all(
            owner_strips.reshape(sub_count, own_pairs, strip_rows, feature_dim),
            "sub",
            split_axis=0,
            concat_axis=2,
            tiled=True,
        ),
        lax.all_to_all(
            partner_strips.reshape(sub_count, own_pairs, strip_rows, feature_dim),
            "sub",
            split_axis=0,
            concat_axis=2,
            tiled=True,
        ),
    )
    left_rows = left_rows.reshape(own_pairs, length, feature_dim)
    right_rows = right_rows.reshape(own_pairs, length, feature_dim)
    rank_limit = lax.dynamic_slice_in_dim(pair_rank[0], first_pair, own_pairs)
    live_pairs = first_pair + jnp.arange(own_pairs, dtype=jnp.int32) < pair_count[0]
    rank_mask = (
        (jnp.arange(sketch_rank, dtype=jnp.int32)[None, :] < rank_limit[:, None])
        & live_pairs[:, None]
    ).astype(jnp.float32)

    def one_pair(pair_item):
        left_pts, right_pts, row_side, col_side, column_mask = pair_item
        kernel_block = kernel_tile(left_pts, right_pts).astype(jnp.bfloat16)
        row_part = jnp.dot(kernel_block, row_side, preferred_element_type=jnp.float32) * column_mask
        col_part = (
            lax.dot_general(
                kernel_block, col_side, (((0,), (0,)), ((), ())), preferred_element_type=jnp.float32
            )
            * column_mask
        )
        return (row_part.astype(jnp.bfloat16), col_part.astype(jnp.bfloat16))

    row_part, col_part = lax.map(
        one_pair, (left_rows, right_rows, row_sketch[0], col_sketch[0], rank_mask)
    )
    row_factor = row_part[None]
    by_rows = lax.all_to_all(
        col_part.reshape(own_pairs, sub_count, strip_rows * sketch_rank),
        "sub",
        split_axis=1,
        concat_axis=0,
        tiled=True,
    )
    placed = lax.dot_general(
        slot_hits.astype(jnp.bfloat16),
        by_rows.reshape(pair_slots, strip_rows * sketch_rank),
        (((0,), (0,)), ((), ())),
        preferred_element_type=jnp.float32,
    ).astype(jnp.bfloat16)
    returned = lax.all_to_all(
        placed.reshape(group_count, CAP * strip_rows * sketch_rank),
        "clu",
        split_axis=0,
        concat_axis=0,
        tiled=True,
    )
    col_factor = returned.reshape(1, group_count, CAP, strip_rows, sketch_rank)
    return (row_factor, col_factor)


def solution(mesh):
    placed = (
        P("clu", "sub", None),
        P("clu", "sub", None, None),
        P("clu", "sub", None, None),
        P("clu"),
        P("clu", None),
        P("clu", None),
        P("clu", None),
        P("clu", None),
    )
    return jax.shard_map(
        shards,
        mesh=mesh,
        in_specs=placed,
        out_specs=(P("clu", "sub", None, None), P("clu", None, None, "sub", None)),
        check_vma=False,
    )
```

profile of v0, /device:TPU:1, one launch (start us, length us, event | category | flops | bytes accessed | tf_op | source)
XLA Modules:
  0.0 476.2 jit_solution(14253315754965208378)
XLA Ops:
  3.5 16.3 %all_to_all.77 = s32[32,1,4]{2,1,0:T(1,128)S(1)} all-to-all(s32[32,1,4]{2,1,0:T(1,128)S(1)} %copy.46), channel_id=1, replica_groups=mesh['clu'=32,'sub'=4] {'clu'}, dimensions={0} | all-to-all | bytes 1024 | tf_op jit(solution)/shard_map/all_to_all | solution.py:12
  20.1 5.1 %convolution_convert_fusion.1 = bf16[64,32768]{1,0:T(8,128)(2,1)} fusion(bf16[4,8,256,128]{3,2,1,0:T(8,128)(2,1)} %bitcast.93, s32[64]{0:T(128)S(1)} %eq.69), kind=kOutput, calls=%fused_computation.25 | convolution fusion | flops 136316928 | bytes 6291712 | tf_op jit(solution)/shard_map/dot_general | solution.py:36
  25.2 10.3 %all_to_all.69 = bf16[32,1,65536]{2,1,0:T(2,128)(2,1)} reshape(bf16[64,32768]{1,0:T(8,128)(2,1)} %convolution_convert_fusion.1) | data formatting | bytes 8388608 | tf_op jit(solution)/shard_map/all_to_all | solution.py:63
  36.1 27.9 %reduce.2 = bf16[32,65536]{1,0:T(8,128)(2,1)} reduce(bf16[32,1,65536]{2,1,0:T(2,128)(2,1)} %all_to_all.69, bf16[]{:T(256)} %broadcast.96), dimensions={1}, to_apply=%all_to_all.69.reduce_sub_computation | reduce | bytes 8388610 | tf_op jit(solution)/shard_map/all_to_all | solution.py:63
  64.0 6.6 %reshape.110 = bf16[32,2,32768]{2,1,0:T(2,128)(2,1)} reshape(bf16[32,65536]{1,0:T(8,128)(2,1)} %reduce.2) | data formatting | bytes 8388608
  70.5 5.2 %all-to-all-start.2 = ((bf16[32,2,32768]{2,1,0:T(2,128)(2,1)}), bf16[32,2,32768]{2,1,0:T(2,128)(2,1)}, u32[]{:S(2)}, u32[]{:S(2)}) async-start(bf16[32,2,32768]{2,1,0:T(2,128)(2,1)} %reshape.110), calls=%async_computation.2 | async-start | bytes 8388608 | tf_op jit(solution)/shard_map/all_to_all | solution.py:63
  78.5 49.6 %all-to-all-done.2 = bf16[32,2,32768]{2,1,0:T(2,128)(2,1)} async-done(((bf16[32,2,32768]{2,1,0:T(2,128)(2,1)}), bf16[32,2,32768]{2,1,0:T(2,128)(2,1)}, u32[]{:S(2)}, u32[]{:S(2)}) %all-to-all-start.2) | async-done | bytes 4194336 | tf_op jit(solution)/shard_map/all_to_all | solution.py:63
  128.0 4.0 all-to-all-start
  132.1 19.8 %reshape.111 = bf16[32,1,65536]{2,1,0:T(2,128)(2,1)} reshape(bf16[32,2,32768]{2,1,0:T(2,128)(2,1)} %all-to-all-done.2) | data formatting | bytes 8388608
  151.8 27.3 %reduce = bf16[32,65536]{1,0:T(8,128)(2,1)} reduce(bf16[32,1,65536]{2,1,0:T(2,128)(2,1)} %reshape.111, bf16[]{:T(256)} %constant.64), dimensions={1}, to_apply=%all_to_all.60.reduce_sub_computation | reduce | bytes 8388610 | tf_op jit(solution)/shard_map/all_to_all | solution.py:63
  179.1 5.4 %reshape.102 = bf16[64,32768]{1,0:T(8,128)(2,1)} reshape(bf16[32,65536]{1,0:T(8,128)(2,1)} %reduce) | data formatting | bytes 8388608 | tf_op jit(solution)/shard_map/reshape | solution.py:72
  184.5 4.3 fusion.26
  188.8 4.4 all-to-all-start.3
  196.0 22.3 %all-to-all-done.3 = bf16[4,8,256,128]{3,1,2,0:T(8,128)(2,1)} async-done(((bf16[4,8,256,128]{3,1,2,0:T(8,128)(2,1)}), bf16[4,8,256,128]{3,1,2,0:T(8,128)(2,1)}, u32[]{:S(2)}, u32[]{:S(2)}) %all-to-all-start.3) | async-done | bytes 2097184 | tf_op jit(solution)/shard_map/all_to_all | solution.py:83
  220.3 65.1 %while.12 = (s32[]{:T(128)}, bf16[8,1024,128]{2,1,0:T(8,128)(2,1)}, bf16[8,1024,128]{2,1,0:T(8,128)(2,1)}, bf16[8,1024,128]{2,1,0:T(8,128)(2,1)}, bf16[8,1024,12...) while((s32[]{:T(128)}, bf16[8,1024,128]{2,1,0:T(8,128)(2,1)}, ...), condition=%wide.region_6.7_spmd, body=%wide.region_3.6_spmd.sunk | while | flops 812906496 | bytes 8410213 | solution.py:112
  289.2 26.5 %all_to_all.78 = bf16[8,4,32768]{2,0,1:T(8,128)(2,1)S(1)} all-to-all(bf16[8,4,32768]{2,0,1:T(8,128)(2,1)S(1)} %copy.51), channel_id=1, replica_groups=mesh['clu'=32,'sub'=4] {'sub'}, dimensions={1} | all-to-all | bytes 4194304 | tf_op jit(solution)/shard_map/all_to_all | solution.py:116
  315.7 3.4 convolution_convert_fusion
  319.1 10.3 %all_to_all.70 = bf16[32,1,65536]{2,1,0:T(2,128)(2,1)} reshape(bf16[64,32768]{1,0:T(8,128)(2,1)} %convolution_convert_fusion) | data formatting | bytes 8388608 | tf_op jit(solution)/shard_map/all_to_all | solution.py:129
  329.4 27.9 %reduce.3 = bf16[32,65536]{1,0:T(8,128)(2,1)} reduce(bf16[32,1,65536]{2,1,0:T(2,128)(2,1)} %all_to_all.70, bf16[]{:T(256)} %broadcast.96), dimensions={1}, to_apply=%all_to_all.70.reduce_sub_computation | reduce | bytes 8388610 | tf_op jit(solution)/shard_map/all_to_all | solution.py:129
  357.3 6.6 %reshape.112 = bf16[32,2,32768]{2,1,0:T(2,128)(2,1)} reshape(bf16[32,65536]{1,0:T(8,128)(2,1)} %reduce.3) | data formatting | bytes 8388608
  363.8 60.2 %all_to_all.79 = bf16[32,2,32768]{2,1,0:T(2,128)(2,1)} all-to-all(bf16[32,2,32768]{2,1,0:T(2,128)(2,1)} %reshape.112), channel_id=1, replica_groups=mesh['clu'=32,'sub'=4] {'clu'}, dimensions={0} | all-to-all | bytes 8388608 | tf_op jit(solution)/shard_map/all_to_all | solution.py:129
  424.0 19.8 %reshape.113 = bf16[32,1,65536]{2,1,0:T(2,128)(2,1)} reshape(bf16[32,2,32768]{2,1,0:T(2,128)(2,1)} %all_to_all.79) | data formatting | bytes 8388608
  443.8 27.2 %reduce.1 = bf16[32,65536]{1,0:T(8,128)(2,1)} reduce(bf16[32,1,65536]{2,1,0:T(2,128)(2,1)} %reshape.113, bf16[]{:T(256)} %constant.64), dimensions={1}, to_apply=%all_to_all.68.reduce_sub_computation | reduce | bytes 8388610 | tf_op jit(solution)/shard_map/all_to_all | solution.py:129
  471.0 5.2 %copy.54 = bf16[4,8,512,128]{3,2,1,0:T(8,128)(2,1)} copy(bf16[4,8,512,128]{3,1,2,0:T(8,128)(2,1)} %bitcast.92) | data formatting | bytes 8388608
  (76 shorter events, 79.1 us)
Async XLA Ops:
  0.6 193.3 %copy-start = (s32[1,32]{1,0:T(1,128)S(1)}, s32[1,32]{1,0:T(1,128)}, u32[]{:S(2)}) copy-start(s32[1,32]{1,0:T(1,128)} %param.17) | copy-start | bytes 388
  70.5 5.2 %copy-start.2 = (bf16[32,256,128]{2,1,0:T(8,128)(2,1)S(1)}, bf16[32,256,128]{2,1,0:T(8,128)(2,1)}, u32[]{:S(2)}) copy-start(bf16[32,256,128]{2,1,0:T(8,128)(2,1)} %param.10) | copy-start | bytes 6291460
  70.5 5.3 %copy-start.3 = (s32[1,32]{1,0:T(1,128)S(1)}, s32[1,32]{1,0:T(1,128)}, u32[]{:S(2)}) copy-start(s32[1,32]{1,0:T(1,128)} %param.14) | copy-start | bytes 388
  70.5 57.5 %all-to-all-start.2 = ((bf16[32,2,32768]{2,1,0:T(2,128)(2,1)}), bf16[32,2,32768]{2,1,0:T(2,128)(2,1)}, u32[]{:S(2)}, u32[]{:S(2)}) async-start(bf16[32,2,32768]{2,1,0:T(2,128)(2,1)} %reshape.110), calls=%async_computation.2 | async-start | bytes 8388608 | tf_op jit(solution)/shard_map/all_to_all | solution.py:63
  128.0 60.8 %all-to-all-start = ((bf16[4,8,256,128]{3,1,2,0:T(8,128)(2,1)}), bf16[4,8,256,128]{3,1,2,0:T(8,128)(2,1)S(1)}, u32[]{:S(2)}, u32[]{:S(2)}) async-start(bf16[4,8,256,128]{3,1,2,0:T(8,128)(2,1)} %fusion.23), calls=%async_computation | async-start | bytes 4194304 | tf_op jit(solution)/shard_map/all_to_all | solution.py:76
  188.8 29.4 %all-to-all-start.3 = ((bf16[4,8,256,128]{3,1,2,0:T(8,128)(2,1)}), bf16[4,8,256,128]{3,1,2,0:T(8,128)(2,1)}, u32[]{:S(2)}, u32[]{:S(2)}) async-start(bf16[4,8,256,128]{3,1,2,0:T(8,128)(2,1)} %fusion.26), calls=%async_computation.3 | async-start | bytes 4194304 | tf_op jit(solution)/shard_map/all_to_all | solution.py:83
  471.0 5.2 %copy-start.1 = (s32[1,32]{1,0:T(1,128)S(1)}, s32[1,32]{1,0:T(1,128)}, u32[]{:S(2)}) copy-start(s32[1,32]{1,0:T(1,128)} %param.17) | copy-start | bytes 388
where the time goes:
time: 480 us; the launch traced here: 476 us
  other arithmetic  123 us (26%)
  blocking collectives  103 us (21%)
  local copies, waits for them, and re-layouts  93.1 us (19%)
  waiting for transfers between devices  71.8 us (15%)
  matrix products  69.9 us (15%)
  starting transfers between devices  13.7 us (3%)
    all_to_all x1, blocking collectives, shards(): lax.all_to_all(placed.reshape(group_count, CAP * strip_rows * sketch_rank...  60.2 us
    unnamed x13, local copies, waits for them, and re-layouts  57.9 us
    all_to_all x2, other arithmetic, shards(): lax.all_to_all(outgoing.reshape(group_count, CAP * strip_rows * feature_d...  55.1 us
    all_to_all x2, other arithmetic, shards(): lax.all_to_all(placed.reshape(group_count, CAP * strip_rows * sketch_rank...  55.1 us
    all_to_all x1, waiting for transfers between devices, shards(): lax.all_to_all(outgoing.reshape(group_count, CAP * strip_rows * feature_d...  49.6 us
    all_to_all x1, blocking collectives, shards(): lax.all_to_all(col_part.reshape(own_pairs, sub_count, strip_rows * sketch...  26.5 us
    all_to_all x1, waiting for transfers between devices, shards(): lax.all_to_all(partner_strips.reshape(sub_count, own_pairs, strip_rows, f...  22.3 us
    dot_general x8, matrix products, one_pair(): lax.dot_general(kernel_block, col_side, (((0,), (0,)), ((), ())), preferr...  19.5 us
  transfers between devices with their start and end apart: 3, of which 2 were waited for; matrix products, arithmetic and copies ran while one was open for 13% of the time, Pallas kernels for 0%

commit v1 on v0

v1 whole, which is shorter than its diff:
```python
import functools

import jax
import jax.numpy as jnp
from jax import lax
from jax.experimental import pallas as pl
from jax.experimental.pallas import tpu as pltpu
from jax.sharding import PartitionSpec as P

CAP = 2
CHUNKS = 4
LOG2E = 1.4426950408889634
MESH = pl.DeviceIdType.MESH


def shift_order(ny, nz, nc):
    near = [(0, 1), (0, 3), (1, 0), (3, 0)]
    diagonal = [(1, 1), (3, 3), (1, 3), (3, 1)]
    far = [(2, 1), (2, 3), (1, 2), (3, 2)]
    straight = [(2, 0), (0, 2), (2, 2)]
    shifts = [(a, b, c) for a, b in straight + far + diagonal + near for c in range(nc)]
    return shifts + [(0, 0, c) for c in range(1, nc)]


def kernel(
    dims,
    idx,
    req,
    points,
    row_sketch,
    col_sketch,
    row_out,
    col_out,
    pts,
    rsk,
    csk,
    asked_v,
    asked_s,
    osend,
    left,
    lnorm,
    acc,
    rowv,
    *rest,
):
    groups, subs, own, strip, rank, chunks = dims
    rows = strip // chunks
    pairs = own * subs
    slots = groups * CAP
    send1, recv1, send2, right, col3, rcol, send4 = (
        rest[k * chunks : (k + 1) * chunks] for k in range(7)
    )
    (
        in_sem,
        out_sem,
        local_sem,
        idx_ssem,
        idx_rsem,
        own_ssem,
        own_rsem,
        far1_ssem,
        far1_rsem,
        x2_ssem,
        x2_rsem,
        x3_ssem,
        x3_rsem,
        far4_ssem,
        far4_rsem,
    ) = rest[7 * chunks :]
    me = lax.axis_index("clu")
    sub = lax.axis_index("sub")
    y, z, core = me // 8, lax.rem(me // 2, 4), lax.rem(me, 2)
    shifts = shift_order(4, 4, 2)
    peers = [
        (lax.rem(y + a, 4) * 4 + lax.rem(z + b, 4)) * 2 + lax.rem(core + c, 2) for a, b, c in shifts
    ]
    turns = [2, 1, 3]
    mates = [lax.rem(sub + k, subs) for k in turns]

    loads = [
        pltpu.make_async_copy(points, pts, in_sem.at[0]),
        pltpu.make_async_copy(row_sketch, rsk, in_sem.at[1]),
        pltpu.make_async_copy(col_sketch, csk, in_sem.at[2]),
    ]
    for copy in loads:
        copy.start()
    barrier = pltpu.get_barrier_semaphore()
    for peer in peers:
        pl.semaphore_signal(barrier, inc=1, device_id={"clu": peer}, device_id_type=MESH)
    for mate in mates:
        pl.semaphore_signal(barrier, inc=1, device_id={"sub": mate}, device_id_type=MESH)
    pl.semaphore_wait(barrier, len(peers) + len(mates))

    pending = []

    def send_clu(src, dst, ssem, rsem, peer):
        copy = pltpu.make_async_remote_copy(
            src_ref=src,
            dst_ref=dst,
            send_sem=ssem,
            recv_sem=rsem,
            device_id={"clu": peer},
            device_id_type=MESH,
        )
        copy.start()
        pending.append(copy)
        return copy

    def send_sub(src, dst, ssem, rsem, mate):
        copy = pltpu.make_async_remote_copy(
            src_ref=src,
            dst_ref=dst,
            send_sem=ssem,
            recv_sem=rsem,
            device_id={"sub": mate},
            device_id_type=MESH,
        )
        copy.start()
        pending.append(copy)
        return copy

    asks = [
        send_clu(req.at[peer], asked_v.at[me], idx_ssem.at[k], idx_rsem.at[k], peer)
        for k, peer in enumerate(peers)
    ]
    asked_v[me] = req[me]

    loads[0].wait()

    def pick_owner(p, carry):
        osend[p // own, lax.rem(p, own)] = pts[idx[pairs + p]]
        return carry

    lax.fori_loop(0, pairs, pick_owner, 0)
    owners = [
        send_sub(osend.at[mate], left.at[sub], own_ssem.at[k], own_rsem.at[k], mate)
        for k, mate in enumerate(mates)
    ]
    left[sub] = osend[sub]

    for copy in asks:
        copy.wait_recv()
    to_scalar = pltpu.make_async_copy(asked_v, asked_s, in_sem.at[3])
    to_scalar.start()
    to_scalar.wait()

    first = []
    for j in range(chunks):

        def pick(t, carry, j=j):
            g = t // CAP
            c = lax.rem(t, CAP)
            send1[j][t] = pts[asked_s[g, 0, c], pl.ds(j * rows, rows)]
            return carry

        lax.fori_loop(0, slots, pick, 0)
        first.append(
            [
                send_clu(
                    send1[j].at[pl.ds(peer * CAP, CAP)],
                    recv1[j].at[pl.ds(me * CAP, CAP)],
                    far1_ssem.at[j, k],
                    far1_rsem.at[j, k],
                    peer,
                )
                for k, peer in enumerate(peers)
            ]
        )
        recv1[j][pl.ds(me * CAP, CAP)] = send1[j][pl.ds(me * CAP, CAP)]
        rcol[j][pairs] = jnp.zeros((rows, rank), jnp.bfloat16)

    for copy in owners:
        copy.wait_recv()
    for copy in loads[1:]:
        copy.wait()

    def norms(i, carry):
        u = left[:, i].reshape(subs * strip, -1).astype(jnp.float32)
        lnorm[i] = lax.dot_general(
            jnp.ones((8, u.shape[1]), jnp.float32),
            u * u * (LOG2E / u.shape[1]),
            (((1,), (1,)), ((), ())),
            precision=lax.Precision.HIGHEST,
            preferred_element_type=jnp.float32,
        )
        return carry

    lax.fori_loop(0, own, norms, 0)

    def forward(j):
        for copy in first[j]:
            copy.wait_recv()

        def pick(p, carry):
            send2[j][p // own, lax.rem(p, own)] = recv1[j][idx[p]]
            return carry

        lax.fori_loop(0, pairs, pick, 0)
        copies = [
            send_sub(
                send2[j].at[mate], right[j].at[sub], x2_ssem.at[j, k], x2_rsem.at[j, k], mate
            )
            for k, mate in enumerate(mates)
        ]
        right[j][sub] = send2[j][sub]
        return copies

    def compute(j, copies):
        for copy in copies:
            copy.wait_recv()

        def one(i, carry):
            u = left[:, i].reshape(subs * strip, -1)
            v = right[j][:, i].reshape(subs * rows, -1)
            width = u.shape[1]
            inner = lax.dot_general(
                v, u, (((1,), (1,)), ((), ())), preferred_element_type=jnp.float32
            )
            wide = v.astype(jnp.float32)
            vnorm = jnp.sum(wide * wide, axis=1, keepdims=True) * (LOG2E / width)
            tile = jnp.exp2(inner * (2.0 * LOG2E / width) - lnorm[i][0:1] - vnorm)
            tile = tile.astype(jnp.bfloat16)
            live = idx[2 * pairs + sub * own + i]
            keep = (lax.broadcasted_iota(jnp.int32, (1, rank), 1) < live).astype(jnp.float32)
            col = jnp.dot(tile, csk[i], preferred_element_type=jnp.float32) * keep
            col3[j][:, i] = col.astype(jnp.bfloat16).reshape(subs, rows, rank)
            side = rsk[i].reshape(subs, strip, rank)[:, j * rows : (j + 1) * rows]
            part = lax.dot_general(
                tile,
                side.reshape(subs * rows, rank),
                (((0,), (0,)), ((), ())),
                preferred_element_type=jnp.float32,
            )
            if j == 0:
                acc[i] = part
            elif j < chunks - 1:
                acc[i] += part
            else:
                rowv[i] = ((acc[i] + part) * keep).astype(jnp.bfloat16)
            return carry

        lax.fori_loop(0, own, one, 0)
        outgoing = [
            send_sub(
                col3[j].at[mate],
                rcol[j].at[pl.ds(sub * own, own)],
                x3_ssem.at[j, k],
                x3_rsem.at[j, k],
                mate,
            )
            for k, mate in enumerate(mates)
        ]
        rcol[j][pl.ds(sub * own, own)] = col3[j][sub]
        return outgoing

    landed = []

    def give_back(j, copies):
        for copy in copies:
            copy.wait_recv()

        def pick(t, carry):
            send4[j][t // CAP, lax.rem(t, CAP)] = rcol[j][idx[3 * pairs + t]]
            return carry

        lax.fori_loop(0, slots, pick, 0)
        place = pl.ds(j * rows, rows)
        for k, peer in enumerate(peers):
            landed.append(
                send_clu(
                    send4[j].at[peer],
                    col_out.at[me, :, place],
                    far4_ssem.at[j, k],
                    far4_rsem.at[j, k],
                    peer,
                )
            )
        mine = pltpu.make_async_copy(send4[j].at[me], col_out.at[me, :, place], local_sem.at[j])
        mine.start()
        return mine

    local = []
    back = None
    for j in range(chunks):
        moved = forward(j)
        if back is not None:
            local.append(give_back(j - 1, back))
        back = compute(j, moved)
    store = pltpu.make_async_copy(rowv, row_out, out_sem)
    store.start()
    local.append(give_back(chunks - 1, back))

    for copy in pending:
        copy.wait_send()
    for copy in landed:
        copy.wait_recv()
    for copy in local:
        copy.wait()
    store.wait()


def shards(
    points, row_sketch, col_sketch, pair_count, pair_local, pair_src, pair_partner, pair_rank
):
    groups = lax.axis_size("clu")
    subs = lax.axis_size("sub")
    clusters, strip, width = points.shape
    pairs = pair_src.shape[1]
    own = pairs // subs
    rank = row_sketch.shape[3]
    chunks = CHUNKS
    rows = strip // chunks
    slots = groups * CAP

    sources = pair_src[0]
    position = jnp.arange(pairs, dtype=jnp.int32)
    earlier = (sources[:, None] == sources[None, :]) & (position[None, :] < position[:, None])
    target = sources * CAP + jnp.sum(earlier.astype(jnp.int32), axis=1)
    hits = target[None, :] == jnp.arange(slots, dtype=jnp.int32)[:, None]
    code = jnp.sum(jnp.where(hits, position * clusters + pair_partner[0] - pairs * clusters, 0), axis=1)
    code = code + pairs * clusters
    named = code // clusters
    wanted = lax.rem(code, clusters)
    live = jnp.where(position < pair_count[0], pair_rank[0], 0)
    idx = jnp.concatenate([target, pair_local[0], live, named])
    req = jnp.pad(wanted.reshape(groups, 1, CAP), ((0, 0), (0, 0), (0, 128 - CAP)))

    per_chunk = [
        ((slots, rows, width), jnp.bfloat16),
        ((slots, rows, width), jnp.bfloat16),
        ((subs, own, rows, width), jnp.bfloat16),
        ((subs, own, rows, width), jnp.bfloat16),
        ((subs, own, rows, rank), jnp.bfloat16),
        ((pairs + 1, rows, rank), jnp.bfloat16),
        ((groups, CAP, rows, rank), jnp.bfloat16),
    ]
    scratch = [
        pltpu.VMEM((clusters, strip, width), jnp.bfloat16),
        pltpu.VMEM((own, subs * strip, rank), jnp.bfloat16),
        pltpu.VMEM((own, subs * strip, rank), jnp.bfloat16),
        pltpu.VMEM((groups, 1, 128), jnp.int32),
        pltpu.SMEM((groups, 1, 128), jnp.int32),
        pltpu.VMEM((subs, own, strip, width), jnp.bfloat16),
        pltpu.VMEM((subs, own, strip, width), jnp.bfloat16),
        pltpu.VMEM((own, 8, subs * strip), jnp.float32),
        pltpu.VMEM((own, subs * strip, rank), jnp.float32),
        pltpu.VMEM((own, subs * strip, rank), jnp.bfloat16),
    ]
    for shape, dtype in per_chunk:
        scratch += [pltpu.VMEM(shape, dtype) for _ in range(chunks)]
    dma = pltpu.SemaphoreType.DMA
    scratch += [
        dma((4,)),
        dma,
        dma((chunks,)),
        dma((groups - 1,)),
        dma((groups - 1,)),
        dma((subs - 1,)),
        dma((subs - 1,)),
        dma((chunks, groups - 1)),
        dma((chunks, groups - 1)),
        dma((chunks, subs - 1)),
        dma((chunks, subs - 1)),
        dma((chunks, subs - 1)),
        dma((chunks, subs - 1)),
        dma((chunks, groups - 1)),
        dma((chunks, groups - 1)),
    ]
    anywhere = pl.BlockSpec(memory_space=pl.ANY)
    row, col = pl.pallas_call(
        functools.partial(kernel, (groups, subs, own, strip, rank, chunks)),
        out_shape=(
            jax.ShapeDtypeStruct((own, subs * strip, rank), jnp.bfloat16),
            jax.ShapeDtypeStruct((groups, CAP, strip, rank), jnp.bfloat16),
        ),
        in_specs=[
            pl.BlockSpec(memory_space=pltpu.SMEM),
            pl.BlockSpec(memory_space=pltpu.VMEM),
            anywhere,
            anywhere,
            anywhere,
        ],
        out_specs=(anywhere, anywhere),
        scratch_shapes=scratch,
        compiler_params=pltpu.CompilerParams(
            collective_id=0, has_side_effects=True, vmem_limit_bytes=56 << 20
        ),
        name="pair_sketches",
    )(idx, req, points, row_sketch[0], col_sketch[0])
    return row[None], col[None]


def solution(mesh):
    placed = (
        P("clu", "sub", None),
        P("clu", "sub", None, None),
        P("clu", "sub", None, None),
        P("clu"),
        P("clu", None),
        P("clu", None),
        P("clu", None),
        P("clu", None),
    )
    return jax.shard_map(
        shards,
        mesh=mesh,
        in_specs=placed,
        out_specs=(P("clu", "sub", None, None), P("clu", None, None, "sub", None)),
        check_vma=False,
    )
```

time: 480 us -> 146 us (0.30)
  Pallas kernels: 0 us -> 134 us
  other arithmetic: 123 us -> 4.34 us
  blocking collectives: 103 us -> 0 us
  local copies, waits for them, and re-layouts: 93.1 us -> 5.94 us
  waiting for transfers between devices: 71.8 us -> 0 us
  matrix products: 69.9 us -> 0 us
  starting transfers between devices: 13.7 us -> 0 us
    pallas_call x0 -> x1, Pallas kernels: none -> 134 us  [shards(): pl.pallas_call(functools.partial(kernel, (groups, subs, own, strip, rank,...]
    all_to_all x5 -> x0, other arithmetic: 110 us -> none  [the longest x2 55.1 us: shards(): lax.all_to_all(outgoing.reshape(group_count, CAP * strip_rows * feature_d...]
    all_to_all x3 -> x0, blocking collectives: 103 us -> none  [the longest x1 60.2 us: shards(): lax.all_to_all(placed.reshape(group_count, CAP * strip_rows * sketch_rank...]
    all_to_all x3 -> x0, waiting for transfers between devices: 71.8 us -> none  [the longest x1 49.6 us: shards(): lax.all_to_all(outgoing.reshape(group_count, CAP * strip_rows * feature_d...]
    dot_general x28 -> x0, matrix products: 69.9 us -> none  [the longest x8 19.5 us: one_pair(): lax.dot_general(kernel_block, col_side, (((0,), (0,)), ((), ())), preferr...]
    unnamed x13 -> x4, local copies, waits for them, and re-layouts: 57.9 us -> 5.23 us
    all_to_all x7 -> x0, local copies, waits for them, and re-layouts: 25.2 us -> none  [the longest x2 10.9 us: shards(): lax.all_to_all(outgoing.reshape(group_count, CAP * strip_rows * feature_d...]
    all_to_all x3 -> x0, starting transfers between devices: 13.7 us -> none  [the longest x1 5.23 us: shards(): lax.all_to_all(outgoing.reshape(group_count, CAP * strip_rows * feature_d...]
  transfers between devices with their start and end apart: 3 -> 0, of which waited for: 2 -> 0; matrix products, arithmetic and copies ran while one was open for 13% -> 0% of each run, Pallas kernels for 0% -> 0%
where the time goes in v1:
time: 146 us
  Pallas kernels  134 us (92%)
  local copies, waits for them, and re-layouts  5.94 us (4%)
  other arithmetic  4.34 us (3%)
    pallas_call x1, Pallas kernels, shards(): pl.pallas_call(functools.partial(kernel, (groups, subs, own, strip, rank,...  134 us
    unnamed x4, local copies, waits for them, and re-layouts  5.23 us

profile of v1, /device:TPU:1, one launch (start us, length us, event | category | flops | bytes accessed | tf_op | source)
XLA Modules:
  0.0 145.6 jit_solution(4739651583103436080)
XLA Ops:
  1.3 0.9 convert_reduce_fusion
  2.2 0.7 fusion.3
  2.9 0.7 compare_select_fusion.2
  3.5 0.7 fusion.2
  4.2 0.1 select_reduce_fusion
  4.3 1.3 pad_add_fusion.idx
  5.6 0.1 add.34
  5.7 0.6 pad.4.req
  6.3 134.0 %pair_sketches.1 = (bf16[8,1024,128]{2,1,0:T(8,128)(2,1)}, bf16[32,2,256,128]{3,2,1,0:T(8,128)(2,1)}) custom-call(s32[160]{0:T(256)} %pad_add_fusion.idx, s32[32,1,128]{2,1,0:T(1,128)} %pad.4.req, bf16[32,256,128]{2,1,0:T(8,128)(2,1)} %points.1, bf16[8,1024,128]{2,1,0:T(8,128)(2,1)} %bitcast.23, bf16[8,1024,128]{2,1,0:T(8,128)(2,1)} %bitcast.24), custom_call_target="tpu_custom_call" | custom-call | tf_op jit(solution)/shard_map/pair_sketches/pallas_call | solution.py:370
  140.4 0.0 copy-start
  140.4 3.2 %copy.22 = bf16[1,8,1024,128]{3,2,1,0:T(8,128)(2,1)} copy(bf16[1,8,1024,128]{3,2,1,0:T(8,128)(2,1)} %bitcast.25) | data formatting | bytes 4194304
  143.6 0.0 copy-done
  143.6 2.0 %copy.23 = bf16[1,32,2,256,128]{4,3,2,1,0:T(8,128)(2,1)} copy(bf16[1,32,2,256,128]{4,3,2,1,0:T(8,128)(2,1)S(1)} %bitcast.22) | data formatting | bytes 8388608
  (2 shorter events, 0.0 us)
Async XLA Ops:
  140.4 3.2 %copy-start = (bf16[32,2,256,128]{3,2,1,0:T(8,128)(2,1)S(1)}, bf16[32,2,256,128]{3,2,1,0:T(8,128)(2,1)}, u32[]{:S(2)}) copy-start(bf16[32,2,256,128]{3,2,1,0:T(8,128)(2,1)} %get-tuple-element.5) | copy-start | bytes 12582916

commit v2 on v1

--- a/solution.py
+++ b/solution.py
@@ -18,14 +18,43 @@
     diagonal = [(1, 1), (3, 3), (1, 3), (3, 1)]
     far = [(2, 1), (2, 3), (1, 2), (3, 2)]
     straight = [(2, 0), (0, 2), (2, 2)]
-    shifts = [(a, b, c) for a, b in straight + far + diagonal + near for c in range(nc)]
+    shifts = [(a, b, c) for c in range(nc) for a, b in straight + far + diagonal + near]
     return shifts + [(0, 0, c) for c in range(1, nc)]
+
+
+def index_tables(count, source, place_of, partner, ranks, table, req):
+    n = source.shape[1]
+    down = lax.broadcasted_iota(jnp.int32, (n, n), 0)
+    along = lax.broadcasted_iota(jnp.int32, (n, n), 1)
+
+    def upright(row):
+        return jnp.sum(jnp.where(down == along, row, 0), axis=1, keepdims=True)
+
+    row = source[...]
+    column = upright(row)
+    same = column == row
+    target = row * CAP + jnp.sum(jnp.where(same & (down < along), 1, 0), axis=0, keepdims=True)
+    upright_target = column * CAP + jnp.sum(
+        jnp.where(same & (along < down), 1, 0), axis=1, keepdims=True
+    )
+    hits = upright_target == lax.broadcasted_iota(jnp.int32, (n, 128), 1)
+    pair = lax.broadcasted_iota(jnp.int32, (n, 128), 0)
+    position = lax.broadcasted_iota(jnp.int32, (1, n), 1)
+    table[...] = jnp.zeros_like(table)
+    table[0, :, 0:n] = target
+    table[1, :, 0:n] = place_of[...]
+    table[2, :, 0:n] = jnp.where(position < count[0], ranks[...], 0)
+    table[3] = jnp.sum(jnp.where(hits, pair - n, 0), axis=0, keepdims=True) + n
+    req[...] = jnp.sum(jnp.where(hits, upright(partner[...]), 0), axis=0, keepdims=True)
 
 
 def kernel(
     dims,
-    idx,
-    req,
+    count,
+    source,
+    place_of,
+    partner,
+    ranks,
     points,
     row_sketch,
     col_sketch,
@@ -34,6 +63,9 @@
     pts,
     rsk,
     csk,
+    table,
+    idx,
+    req,
     asked_v,
     asked_s,
     osend,
@@ -89,6 +121,9 @@
         pl.semaphore_signal(barrier, inc=1, device_id={"clu": peer}, device_id_type=MESH)
     for mate in mates:
         pl.semaphore_signal(barrier, inc=1, device_id={"sub": mate}, device_id_type=MESH)
+    index_tables(count, source, place_of, partner, ranks, table, req)
+    to_scalar = pltpu.make_async_copy(table, idx, in_sem.at[3])
+    to_scalar.start()
     pl.semaphore_wait(barrier, len(peers) + len(mates))
 
     pending = []
@@ -120,15 +155,16 @@
         return copy
 
     asks = [
-        send_clu(req.at[peer], asked_v.at[me], idx_ssem.at[k], idx_rsem.at[k], peer)
+        send_clu(req, asked_v.at[me], idx_ssem.at[k], idx_rsem.at[k], peer)
         for k, peer in enumerate(peers)
     ]
-    asked_v[me] = req[me]
+    asked_v[me] = req[...]
+    to_scalar.wait()
 
     loads[0].wait()
 
     def pick_owner(p, carry):
-        osend[p // own, lax.rem(p, own)] = pts[idx[pairs + p]]
+        osend[p // own, lax.rem(p, own)] = pts[idx[1, 0, p]]
         return carry
 
     lax.fori_loop(0, pairs, pick_owner, 0)
@@ -140,73 +176,70 @@
 
     for copy in asks:
         copy.wait_recv()
-    to_scalar = pltpu.make_async_copy(asked_v, asked_s, in_sem.at[3])
+    to_scalar = pltpu.make_async_copy(asked_v, asked_s, in_sem.at[4])
     to_scalar.start()
     to_scalar.wait()
 
-    first = []
-    for j in range(chunks):
-
-        def pick(t, carry, j=j):
-            g = t // CAP
-            c = lax.rem(t, CAP)
-            send1[j][t] = pts[asked_s[g, 0, c], pl.ds(j * rows, rows)]
+    first, moved, back, landed, local = {}, {}, {}, [], []
+
+    def launch(j):
+        def pick(t, carry):
+            wanted = asked_s[t // CAP, 0, me * CAP + lax.rem(t, CAP)]
+            send1[j][t] = pts[wanted, pl.ds(j * rows, rows)]
             return carry
 
         lax.fori_loop(0, slots, pick, 0)
-        first.append(
-            [
-                send_clu(
-                    send1[j].at[pl.ds(peer * CAP, CAP)],
-                    recv1[j].at[pl.ds(me * CAP, CAP)],
-                    far1_ssem.at[j, k],
-                    far1_rsem.at[j, k],
-                    peer,
-                )
-                for k, peer in enumerate(peers)
-            ]
-        )
+        first[j] = [
+            send_clu(
+                send1[j].at[pl.ds(peer * CAP, CAP)],
+                recv1[j].at[pl.ds(me * CAP, CAP)],
+                far1_ssem.at[j, k],
+                far1_rsem.at[j, k],
+                peer,
+            )
+            for k, peer in enumerate(peers)
+        ]
         recv1[j][pl.ds(me * CAP, CAP)] = send1[j][pl.ds(me * CAP, CAP)]
         rcol[j][pairs] = jnp.zeros((rows, rank), jnp.bfloat16)
 
-    for copy in owners:
-        copy.wait_recv()
-    for copy in loads[1:]:
-        copy.wait()
-
-    def norms(i, carry):
-        u = left[:, i].reshape(subs * strip, -1).astype(jnp.float32)
-        lnorm[i] = lax.dot_general(
-            jnp.ones((8, u.shape[1]), jnp.float32),
-            u * u * (LOG2E / u.shape[1]),
-            (((1,), (1,)), ((), ())),
-            precision=lax.Precision.HIGHEST,
-            preferred_element_type=jnp.float32,
-        )
-        return carry
-
-    lax.fori_loop(0, own, norms, 0)
+    def norms():
+        for copy in owners:
+            copy.wait_recv()
+        for copy in loads[1:]:
+            copy.wait()
+
+        def norms_of(i, carry):
+            u = left[:, i].reshape(subs * strip, -1).astype(jnp.float32)
+            lnorm[i] = lax.dot_general(
+                jnp.ones((8, u.shape[1]), jnp.float32),
+                u * u * (LOG2E / u.shape[1]),
+                (((1,), (1,)), ((), ())),
+                precision=lax.Precision.HIGHEST,
+                preferred_element_type=jnp.float32,
+            )
+            return carry
+
+        lax.fori_loop(0, own, norms_of, 0)
 
     def forward(j):
         for copy in first[j]:
             copy.wait_recv()
 
         def pick(p, carry):
-            send2[j][p // own, lax.rem(p, own)] = recv1[j][idx[p]]
+            send2[j][p // own, lax.rem(p, own)] = recv1[j][idx[0, 0, p]]
             return carry
 
         lax.fori_loop(0, pairs, pick, 0)
-        copies = [
+        moved[j] = [
             send_sub(
                 send2[j].at[mate], right[j].at[sub], x2_ssem.at[j, k], x2_rsem.at[j, k], mate
             )
             for k, mate in enumerate(mates)
         ]
         right[j][sub] = send2[j][sub]
-        return copies
-
-    def compute(j, copies):
-        for copy in copies:
+
+    def compute(j):
+        for copy in moved[j]:
             copy.wait_recv()
 
         def one(i, carry):
@@ -220,7 +253,7 @@
             vnorm = jnp.sum(wide * wide, axis=1, keepdims=True) * (LOG2E / width)
             tile = jnp.exp2(inner * (2.0 * LOG2E / width) - lnorm[i][0:1] - vnorm)
             tile = tile.astype(jnp.bfloat16)
-            live = idx[2 * pairs + sub * own + i]
+            live = idx[2, 0, sub * own + i]
             keep = (lax.broadcasted_iota(jnp.int32, (1, rank), 1) < live).astype(jnp.float32)
             col = jnp.dot(tile, csk[i], preferred_element_type=jnp.float32) * keep
             col3[j][:, i] = col.astype(jnp.bfloat16).reshape(subs, rows, rank)
@@ -240,7 +273,7 @@
             return carry
 
         lax.fori_loop(0, own, one, 0)
-        outgoing = [
+        back[j] = [
             send_sub(
                 col3[j].at[mate],
                 rcol[j].at[pl.ds(sub * own, own)],
@@ -251,16 +284,13 @@
             for k, mate in enumerate(mates)
         ]
         rcol[j][pl.ds(sub * own, own)] = col3[j][sub]
-        return outgoing
-
-    landed = []
-
-    def give_back(j, copies):
-        for copy in copies:
+
+    def give_back(j):
+        for copy in back[j]:
             copy.wait_recv()
 
         def pick(t, carry):
-            send4[j][t // CAP, lax.rem(t, CAP)] = rcol[j][idx[3 * pairs + t]]
+            send4[j][t // CAP, lax.rem(t, CAP)] = rcol[j][idx[3, 0, t]]
             return carry
 
         lax.fori_loop(0, slots, pick, 0)
@@ -277,18 +307,21 @@
             )
         mine = pltpu.make_async_copy(send4[j].at[me], col_out.at[me, :, place], local_sem.at[j])
         mine.start()
-        return mine
-
-    local = []
-    back = None
+        local.append(mine)
+
     for j in range(chunks):
-        moved = forward(j)
-        if back is not None:
-            local.append(give_back(j - 1, back))
-        back = compute(j, moved)
+        launch(j)
+    norms()
+    forward(0)
+    for j in range(chunks):
+        if j + 1 < chunks:
+            forward(j + 1)
+        compute(j)
+        if j > 0:
+            give_back(j - 1)
     store = pltpu.make_async_copy(rowv, row_out, out_sem)
     store.start()
-    local.append(give_back(chunks - 1, back))
+    give_back(chunks - 1)
 
     for copy in pending:
         copy.wait_send()
@@ -312,19 +345,6 @@
     rows = strip // chunks
     slots = groups * CAP
 
-    sources = pair_src[0]
-    position = jnp.arange(pairs, dtype=jnp.int32)
-    earlier = (sources[:, None] == sources[None, :]) & (position[None, :] < position[:, None])
-    target = sources * CAP + jnp.sum(earlier.astype(jnp.int32), axis=1)
-    hits = target[None, :] == jnp.arange(slots, dtype=jnp.int32)[:, None]
-    code = jnp.sum(jnp.where(hits, position * clusters + pair_partner[0] - pairs * clusters, 0), axis=1)
-    code = code + pairs * clusters
-    named = code // clusters
-    wanted = lax.rem(code, clusters)
-    live = jnp.where(position < pair_count[0], pair_rank[0], 0)
-    idx = jnp.concatenate([target, pair_local[0], live, named])
-    req = jnp.pad(wanted.reshape(groups, 1, CAP), ((0, 0), (0, 0), (0, 128 - CAP)))
-
     per_chunk = [
         ((slots, rows, width), jnp.bfloat16),
         ((slots, rows, width), jnp.bfloat16),
@@ -338,6 +358,9 @@
         pltpu.VMEM((clusters, strip, width), jnp.bfloat16),
         pltpu.VMEM((own, subs * strip, rank), jnp.bfloat16),
         pltpu.VMEM((own, subs * strip, rank), jnp.bfloat16),
+        pltpu.VMEM((4, 1, 128), jnp.int32),
+        pltpu.SMEM((4, 1, 128), jnp.int32),
+        pltpu.VMEM((1, 128), jnp.int32),
         pltpu.VMEM((groups, 1, 128), jnp.int32),
         pltpu.SMEM((groups, 1, 128), jnp.int32),
         pltpu.VMEM((subs, own, strip, width), jnp.bfloat16),
@@ -350,7 +373,7 @@
         scratch += [pltpu.VMEM(shape, dtype) for _ in range(chunks)]
     dma = pltpu.SemaphoreType.DMA
     scratch += [
-        dma((4,)),
+        dma((5,)),
         dma,
         dma((chunks,)),
         dma((groups - 1,)),
@@ -366,6 +389,7 @@
         dma((chunks, groups - 1)),
         dma((chunks, groups - 1)),
     ]
+    small = pl.BlockSpec(memory_space=pltpu.VMEM)
     anywhere = pl.BlockSpec(memory_space=pl.ANY)
     row, col = pl.pallas_call(
         functools.partial(kernel, (groups, subs, own, strip, rank, chunks)),
@@ -375,7 +399,10 @@
         ),
         in_specs=[
             pl.BlockSpec(memory_space=pltpu.SMEM),
-            pl.BlockSpec(memory_space=pltpu.VMEM),
+            small,
+            small,
+            small,
+            small,
             anywhere,
             anywhere,
             anywhere,
@@ -386,7 +413,16 @@
             collective_id=0, has_side_effects=True, vmem_limit_bytes=56 << 20
         ),
         name="pair_sketches",
-    )(idx, req, points, row_sketch[0], col_sketch[0])
+    )(
+        pair_count,
+        pair_src,
+        pair_local,
+        pair_partner,
+        pair_rank,
+        points,
+        row_sketch[0],
+        col_sketch[0],
+    )
     return row[None], col[None]
 
 

time: 146 us -> 121 us (0.83)
  Pallas kernels: 134 us -> 115 us
  other arithmetic: 4.34 us -> 0 us
    pallas_call x1, Pallas kernels: 134 us -> 115 us  [shards(): pl.pallas_call(functools.partial(kernel, (groups, subs, own, strip, rank,...]
where the time goes in v2:
time: 121 us
  Pallas kernels  115 us (95%)
  local copies, waits for them, and re-layouts  5.23 us (4%)
  between operations  1.29 us (1%)
    pallas_call x1, Pallas kernels, shards(): pl.pallas_call(functools.partial(kernel, (groups, subs, own, strip, rank,...  115 us
    unnamed x4, local copies, waits for them, and re-layouts  5.23 us

profile of v2, /device:TPU:1, one launch (start us, length us, event | category | flops | bytes accessed | tf_op | source)
XLA Modules:
  0.0 121.2 jit_solution(2477487064123216514)
XLA Ops:
  1.3 114.7 %pair_sketches.1 = (bf16[8,1024,128]{2,1,0:T(8,128)(2,1)}, bf16[32,2,256,128]{3,2,1,0:T(8,128)(2,1)}) custom-call(s32[1]{0:T(128)S(6)} %copy.12.count, s32[1,32]{1,0:T(1,128)} %source.1, s32[1,32]{1,0:T(1,128)} %place_of.1, s32[1,32]{1,0:T(1,128)} %partner.1, s32[1,32]{1,0:T(1,128)} %ranks.1, bf16[32,256,128]{2,1,0:T(8,128)(2,1)} %points.1, ...), custom_call_target="tpu_custom_call" | custom-call | tf_op jit(solution)/shard_map/pair_sketches/pallas_call | solution.py:394
  116.0 0.0 copy-start
  116.0 3.2 %copy.13 = bf16[1,8,1024,128]{3,2,1,0:T(8,128)(2,1)} copy(bf16[1,8,1024,128]{3,2,1,0:T(8,128)(2,1)} %bitcast.7) | data formatting | bytes 4194304
  119.2 0.0 copy-done
  119.2 2.0 %copy.14 = bf16[1,32,2,256,128]{4,3,2,1,0:T(8,128)(2,1)} copy(bf16[1,32,2,256,128]{4,3,2,1,0:T(8,128)(2,1)S(1)} %bitcast.4) | data formatting | bytes 8388608
Async XLA Ops:
  116.0 3.2 %copy-start = (bf16[32,2,256,128]{3,2,1,0:T(8,128)(2,1)S(1)}, bf16[32,2,256,128]{3,2,1,0:T(8,128)(2,1)}, u32[]{:S(2)}) copy-start(bf16[32,2,256,128]{3,2,1,0:T(8,128)(2,1)} %get-tuple-element.5) | copy-start | bytes 12582916

commit v3 on v2

--- a/solution.py
+++ b/solution.py
@@ -124,63 +124,44 @@
     index_tables(count, source, place_of, partner, ranks, table, req)
     to_scalar = pltpu.make_async_copy(table, idx, in_sem.at[3])
     to_scalar.start()
+    to_scalar.wait()
+    loads[0].wait()
+
+    def pick_owner(p, carry):
+        osend[p // own, lax.rem(p, own)] = pts[idx[1, 0, p]]
+        return carry
+
+    lax.fori_loop(0, pairs, pick_owner, 0)
     pl.semaphore_wait(barrier, len(peers) + len(mates))
 
-    pending = []
-
-    def send_clu(src, dst, ssem, rsem, peer):
-        copy = pltpu.make_async_remote_copy(
+    def send(src, dst, ssem, rsem, axis, to):
+        pltpu.make_async_remote_copy(
             src_ref=src,
             dst_ref=dst,
             send_sem=ssem,
             recv_sem=rsem,
-            device_id={"clu": peer},
+            device_id={axis: to},
             device_id_type=MESH,
-        )
-        copy.start()
-        pending.append(copy)
-        return copy
-
-    def send_sub(src, dst, ssem, rsem, mate):
-        copy = pltpu.make_async_remote_copy(
-            src_ref=src,
-            dst_ref=dst,
-            send_sem=ssem,
-            recv_sem=rsem,
-            device_id={"sub": mate},
-            device_id_type=MESH,
-        )
-        copy.start()
-        pending.append(copy)
-        return copy
-
-    asks = [
-        send_clu(req, asked_v.at[me], idx_ssem.at[k], idx_rsem.at[k], peer)
-        for k, peer in enumerate(peers)
-    ]
+        ).start()
+
+    def await_all(ref, count, sem):
+        blocks = ref.at[pl.ds(0, count)]
+        pltpu.make_async_copy(blocks, blocks, sem).wait()
+
+    for peer in peers:
+        send(req, asked_v.at[me], idx_ssem, idx_rsem, "clu", peer)
     asked_v[me] = req[...]
-    to_scalar.wait()
-
-    loads[0].wait()
-
-    def pick_owner(p, carry):
-        osend[p // own, lax.rem(p, own)] = pts[idx[1, 0, p]]
-        return carry
-
-    lax.fori_loop(0, pairs, pick_owner, 0)
-    owners = [
-        send_sub(osend.at[mate], left.at[sub], own_ssem.at[k], own_rsem.at[k], mate)
-        for k, mate in enumerate(mates)
-    ]
+
+    for mate in mates:
+        send(osend.at[mate], left.at[sub], own_ssem, own_rsem, "sub", mate)
     left[sub] = osend[sub]
 
-    for copy in asks:
-        copy.wait_recv()
+    await_all(asked_v, groups - 1, idx_rsem)
     to_scalar = pltpu.make_async_copy(asked_v, asked_s, in_sem.at[4])
     to_scalar.start()
     to_scalar.wait()
 
-    first, moved, back, landed, local = {}, {}, {}, [], []
+    local = []
 
     def launch(j):
         def pick(t, carry):
@@ -189,22 +170,20 @@
             return carry
 
         lax.fori_loop(0, slots, pick, 0)
-        first[j] = [
-            send_clu(
+        for peer in peers:
+            send(
                 send1[j].at[pl.ds(peer * CAP, CAP)],
                 recv1[j].at[pl.ds(me * CAP, CAP)],
-                far1_ssem.at[j, k],
-                far1_rsem.at[j, k],
+                far1_ssem.at[j],
+                far1_rsem.at[j],
+                "clu",
                 peer,
             )
-            for k, peer in enumerate(peers)
-        ]
         recv1[j][pl.ds(me * CAP, CAP)] = send1[j][pl.ds(me * CAP, CAP)]
         rcol[j][pairs] = jnp.zeros((rows, rank), jnp.bfloat16)
 
     def norms():
-        for copy in owners:
-            copy.wait_recv()
+        await_all(left, subs - 1, own_rsem)
         for copy in loads[1:]:
             copy.wait()
 
@@ -222,25 +201,19 @@
         lax.fori_loop(0, own, norms_of, 0)
 
     def forward(j):
-        for copy in first[j]:
-            copy.wait_recv()
+        await_all(recv1[j], slots - CAP, far1_rsem.at[j])
 
         def pick(p, carry):
             send2[j][p // own, lax.rem(p, own)] = recv1[j][idx[0, 0, p]]
             return carry
 
         lax.fori_loop(0, pairs, pick, 0)
-        moved[j] = [
-            send_sub(
-                send2[j].at[mate], right[j].at[sub], x2_ssem.at[j, k], x2_rsem.at[j, k], mate
-            )
-            for k, mate in enumerate(mates)
-        ]
+        for mate in mates:
+            send(send2[j].at[mate], right[j].at[sub], x2_ssem.at[j], x2_rsem.at[j], "sub", mate)
         right[j][sub] = send2[j][sub]
 
     def compute(j):
-        for copy in moved[j]:
-            copy.wait_recv()
+        await_all(right[j], subs - 1, x2_rsem.at[j])
 
         def one(i, carry):
             u = left[:, i].reshape(subs * strip, -1)
@@ -273,21 +246,19 @@
             return carry
 
         lax.fori_loop(0, own, one, 0)
-        back[j] = [
-            send_sub(
+        for mate in mates:
+            send(
                 col3[j].at[mate],
                 rcol[j].at[pl.ds(sub * own, own)],
-                x3_ssem.at[j, k],
-                x3_rsem.at[j, k],
+                x3_ssem.at[j],
+                x3_rsem.at[j],
+                "sub",
                 mate,
             )
-            for k, mate in enumerate(mates)
-        ]
         rcol[j][pl.ds(sub * own, own)] = col3[j][sub]
 
     def give_back(j):
-        for copy in back[j]:
-            copy.wait_recv()
+        await_all(rcol[j], pairs - own, x3_rsem.at[j])
 
         def pick(t, carry):
             send4[j][t // CAP, lax.rem(t, CAP)] = rcol[j][idx[3, 0, t]]
@@ -295,15 +266,14 @@
 
         lax.fori_loop(0, slots, pick, 0)
         place = pl.ds(j * rows, rows)
-        for k, peer in enumerate(peers):
-            landed.append(
-                send_clu(
-                    send4[j].at[peer],
-                    col_out.at[me, :, place],
-                    far4_ssem.at[j, k],
-                    far4_rsem.at[j, k],
-                    peer,
-                )
+        for peer in peers:
+            send(
+                send4[j].at[peer],
+                col_out.at[me, :, place],
+                far4_ssem.at[j],
+                far4_rsem,
+                "clu",
+                peer,
             )
         mine = pltpu.make_async_copy(send4[j].at[me], col_out.at[me, :, place], local_sem.at[j])
         mine.start()
@@ -323,10 +293,14 @@
     store.start()
     give_back(chunks - 1)
 
-    for copy in pending:
-        copy.wait_send()
-    for copy in landed:
-        copy.wait_recv()
+    await_all(asked_v, groups - 1, idx_ssem)
+    await_all(left, subs - 1, own_ssem)
+    for j in range(chunks):
+        await_all(send1[j], slots - CAP, far1_ssem.at[j])
+        await_all(send2[j], subs - 1, x2_ssem.at[j])
+        await_all(col3[j], subs - 1, x3_ssem.at[j])
+        await_all(send4[j], groups - 1, far4_ssem.at[j])
+    await_all(col_out, groups - 1, far4_rsem)
     for copy in local:
         copy.wait()
     store.wait()
@@ -376,18 +350,18 @@
         dma((5,)),
         dma,
         dma((chunks,)),
-        dma((groups - 1,)),
-        dma((groups - 1,)),
-        dma((subs - 1,)),
-        dma((subs - 1,)),
-        dma((chunks, groups - 1)),
-        dma((chunks, groups - 1)),
-        dma((chunks, subs - 1)),
-        dma((chunks, subs - 1)),
-        dma((chunks, subs - 1)),
-        dma((chunks, subs - 1)),
-        dma((chunks, groups - 1)),
-        dma((chunks, groups - 1)),
+        dma,
+        dma,
+        dma,
+        dma,
+        dma((chunks,)),
+        dma((chunks,)),
+        dma((chunks,)),
+        dma((chunks,)),
+        dma((chunks,)),
+        dma((chunks,)),
+        dma((chunks,)),
+        dma,
     ]
     small = pl.BlockSpec(memory_space=pltpu.VMEM)
     anywhere = pl.BlockSpec(memory_space=pl.ANY)

time: 121 us -> 116 us (0.959)
  Pallas kernels: 115 us -> 109 us
    pallas_call x1, Pallas kernels: 115 us -> 109 us  [shards(): pl.pallas_call(functools.partial(kernel, (groups, subs, own, strip, rank,...]
where the time goes in v3:
time: 116 us
  Pallas kernels  109 us (94%)
  local copies, waits for them, and re-layouts  5.23 us (5%)
  between operations  1.29 us (1%)
    pallas_call x1, Pallas kernels, shards(): pl.pallas_call(functools.partial(kernel, (groups, subs, own, strip, rank,...  109 us
    unnamed x4, local copies, waits for them, and re-layouts  5.23 us

profile of v3, /device:TPU:1, one launch (start us, length us, event | category | flops | bytes accessed | tf_op | source)
XLA Modules:
  0.0 115.5 jit_solution(7621138574783423545)
XLA Ops:
  1.3 109.0 %pair_sketches.1 = (bf16[8,1024,128]{2,1,0:T(8,128)(2,1)}, bf16[32,2,256,128]{3,2,1,0:T(8,128)(2,1)}) custom-call(s32[1]{0:T(128)S(6)} %copy.12.count, s32[1,32]{1,0:T(1,128)} %source.1, s32[1,32]{1,0:T(1,128)} %place_of.1, s32[1,32]{1,0:T(1,128)} %partner.1, s32[1,32]{1,0:T(1,128)} %ranks.1, bf16[32,256,128]{2,1,0:T(8,128)(2,1)} %points.1, ...), custom_call_target="tpu_custom_call" | custom-call | tf_op jit(solution)/shard_map/pair_sketches/pallas_call | solution.py:368
  110.3 0.0 copy-start
  110.3 3.2 %copy.13 = bf16[1,8,1024,128]{3,2,1,0:T(8,128)(2,1)} copy(bf16[1,8,1024,128]{3,2,1,0:T(8,128)(2,1)} %bitcast.7) | data formatting | bytes 4194304
  113.5 0.0 copy-done
  113.5 2.0 %copy.14 = bf16[1,32,2,256,128]{4,3,2,1,0:T(8,128)(2,1)} copy(bf16[1,32,2,256,128]{4,3,2,1,0:T(8,128)(2,1)S(1)} %bitcast.4) | data formatting | bytes 8388608
Async XLA Ops:
  110.3 3.2 %copy-start = (bf16[32,2,256,128]{3,2,1,0:T(8,128)(2,1)S(1)}, bf16[32,2,256,128]{3,2,1,0:T(8,128)(2,1)}, u32[]{:S(2)}) copy-start(bf16[32,2,256,128]{3,2,1,0:T(8,128)(2,1)} %get-tuple-element.5) | copy-start | bytes 12582916

commit v4 on v3

--- a/solution.py
+++ b/solution.py
@@ -51,10 +51,10 @@
 def kernel(
     dims,
     count,
-    source,
-    place_of,
-    partner,
-    ranks,
+    source_in,
+    place_in,
+    partner_in,
+    ranks_in,
     points,
     row_sketch,
     col_sketch,
@@ -63,6 +63,10 @@
     pts,
     rsk,
     csk,
+    source,
+    place_of,
+    partner,
+    ranks,
     table,
     idx,
     req,
@@ -114,13 +118,21 @@
         pltpu.make_async_copy(row_sketch, rsk, in_sem.at[1]),
         pltpu.make_async_copy(col_sketch, csk, in_sem.at[2]),
     ]
-    for copy in loads:
+    lists = [
+        pltpu.make_async_copy(given, held, in_sem.at[5 + k])
+        for k, (given, held) in enumerate(
+            [(source_in, source), (place_in, place_of), (partner_in, partner), (ranks_in, ranks)]
+        )
+    ]
+    for copy in lists + loads:
         copy.start()
     barrier = pltpu.get_barrier_semaphore()
     for peer in peers:
         pl.semaphore_signal(barrier, inc=1, device_id={"clu": peer}, device_id_type=MESH)
     for mate in mates:
         pl.semaphore_signal(barrier, inc=1, device_id={"sub": mate}, device_id_type=MESH)
+    for copy in lists:
+        copy.wait()
     index_tables(count, source, place_of, partner, ranks, table, req)
     to_scalar = pltpu.make_async_copy(table, idx, in_sem.at[3])
     to_scalar.start()
@@ -164,13 +176,12 @@
     local = []
 
     def launch(j):
-        def pick(t, carry):
-            wanted = asked_s[t // CAP, 0, me * CAP + lax.rem(t, CAP)]
-            send1[j][t] = pts[wanted, pl.ds(j * rows, rows)]
-            return carry
-
-        lax.fori_loop(0, slots, pick, 0)
+        def wanted(group, c):
+            return pts[asked_s[group, 0, me * CAP + c], pl.ds(j * rows, rows)]
+
         for peer in peers:
+            for c in range(CAP):
+                send1[j][peer * CAP + c] = wanted(peer, c)
             send(
                 send1[j].at[pl.ds(peer * CAP, CAP)],
                 recv1[j].at[pl.ds(me * CAP, CAP)],
@@ -179,7 +190,8 @@
                 "clu",
                 peer,
             )
-        recv1[j][pl.ds(me * CAP, CAP)] = send1[j][pl.ds(me * CAP, CAP)]
+        for c in range(CAP):
+            recv1[j][me * CAP + c] = wanted(me, c)
         rcol[j][pairs] = jnp.zeros((rows, rank), jnp.bfloat16)
 
     def norms():
@@ -260,13 +272,10 @@
     def give_back(j):
         await_all(rcol[j], pairs - own, x3_rsem.at[j])
 
-        def pick(t, carry):
-            send4[j][t // CAP, lax.rem(t, CAP)] = rcol[j][idx[3, 0, t]]
-            return carry
-
-        lax.fori_loop(0, slots, pick, 0)
         place = pl.ds(j * rows, rows)
         for peer in peers:
+            for c in range(CAP):
+                send4[j][peer, c] = rcol[j][idx[3, 0, peer * CAP + c]]
             send(
                 send4[j].at[peer],
                 col_out.at[me, :, place],
@@ -275,6 +284,8 @@
                 "clu",
                 peer,
             )
+        for c in range(CAP):
+            send4[j][me, c] = rcol[j][idx[3, 0, me * CAP + c]]
         mine = pltpu.make_async_copy(send4[j].at[me], col_out.at[me, :, place], local_sem.at[j])
         mine.start()
         local.append(mine)
@@ -332,6 +343,10 @@
         pltpu.VMEM((clusters, strip, width), jnp.bfloat16),
         pltpu.VMEM((own, subs * strip, rank), jnp.bfloat16),
         pltpu.VMEM((own, subs * strip, rank), jnp.bfloat16),
+        pltpu.VMEM((1, pairs), jnp.int32),
+        pltpu.VMEM((1, pairs), jnp.int32),
+        pltpu.VMEM((1, pairs), jnp.int32),
+        pltpu.VMEM((1, pairs), jnp.int32),
         pltpu.VMEM((4, 1, 128), jnp.int32),
         pltpu.SMEM((4, 1, 128), jnp.int32),
         pltpu.VMEM((1, 128), jnp.int32),
@@ -347,23 +362,22 @@
         scratch += [pltpu.VMEM(shape, dtype) for _ in range(chunks)]
     dma = pltpu.SemaphoreType.DMA
     scratch += [
-        dma((5,)),
-        dma,
-        dma((chunks,)),
-        dma,
-        dma,
-        dma,
-        dma,
-        dma((chunks,)),
-        dma((chunks,)),
-        dma((chunks,)),
-        dma((chunks,)),
-        dma((chunks,)),
-        dma((chunks,)),
-        dma((chunks,)),
-        dma,
-    ]
-    small = pl.BlockSpec(memory_space=pltpu.VMEM)
+        dma((9,)),
+        dma,
+        dma((chunks,)),
+        dma,
+        dma,
+        dma,
+        dma,
+        dma((chunks,)),
+        dma((chunks,)),
+        dma((chunks,)),
+        dma((chunks,)),
+        dma((chunks,)),
+        dma((chunks,)),
+        dma((chunks,)),
+        dma,
+    ]
     anywhere = pl.BlockSpec(memory_space=pl.ANY)
     row, col = pl.pallas_call(
         functools.partial(kernel, (groups, subs, own, strip, rank, chunks)),
@@ -373,10 +387,10 @@
         ),
         in_specs=[
             pl.BlockSpec(memory_space=pltpu.SMEM),
-            small,
-            small,
-            small,
-            small,
+            anywhere,
+            anywhere,
+            anywhere,
+            anywhere,
             anywhere,
             anywhere,
             anywhere,

time: 116 us -> 114 us (0.983)
    pallas_call x1, Pallas kernels: 109 us -> 108 us  [shards(): pl.pallas_call(functools.partial(kernel, (groups, subs, own, strip, rank,...]
where the time goes in v4:
time: 114 us
  Pallas kernels  108 us (95%)
  local copies, waits for them, and re-layouts  5.23 us (5%)
  between operations  1.29 us (1%)
    pallas_call x1, Pallas kernels, shards(): pl.pallas_call(functools.partial(kernel, (groups, subs, own, strip, rank,...  108 us
    unnamed x4, local copies, waits for them, and re-layouts  5.23 us

profile of v4, /device:TPU:1, one launch (start us, length us, event | category | flops | bytes accessed | tf_op | source)
XLA Modules:
  0.0 114.3 jit_solution(1112278230951798636)
XLA Ops:
  1.3 107.8 %pair_sketches.1 = (bf16[8,1024,128]{2,1,0:T(8,128)(2,1)}, bf16[32,2,256,128]{3,2,1,0:T(8,128)(2,1)}) custom-call(s32[1]{0:T(128)S(6)} %copy.12.count, s32[1,32]{1,0:T(1,128)} %source_in.1, s32[1,32]{1,0:T(1,128)} %place_in.1, s32[1,32]{1,0:T(1,128)} %partner_in.1, s32[1,32]{1,0:T(1,128)} %ranks_in.1, bf16[32,256,128]{2,1,0:T(8,128)(2,1)} %points.1, ...), custom_call_target="tpu_custom_call" | custom-call | tf_op jit(solution)/shard_map/pair_sketches/pallas_call | solution.py:382
  109.1 0.0 copy-start
  109.1 3.2 %copy.13 = bf16[1,8,1024,128]{3,2,1,0:T(8,128)(2,1)} copy(bf16[1,8,1024,128]{3,2,1,0:T(8,128)(2,1)} %bitcast.7) | data formatting | bytes 4194304
  112.3 0.0 copy-done
  112.3 2.0 %copy.14 = bf16[1,32,2,256,128]{4,3,2,1,0:T(8,128)(2,1)} copy(bf16[1,32,2,256,128]{4,3,2,1,0:T(8,128)(2,1)S(1)} %bitcast.4) | data formatting | bytes 8388608
Async XLA Ops:
  109.1 3.2 %copy-start = (bf16[32,2,256,128]{3,2,1,0:T(8,128)(2,1)S(1)}, bf16[32,2,256,128]{3,2,1,0:T(8,128)(2,1)}, u32[]{:S(2)}) copy-start(bf16[32,2,256,128]{3,2,1,0:T(8,128)(2,1)} %get-tuple-element.5) | copy-start | bytes 12582916

commit v5 on v4

--- a/solution.py
+++ b/solution.py
@@ -8,7 +8,7 @@
 from jax.sharding import PartitionSpec as P
 
 CAP = 2
-CHUNKS = 4
+CHUNKS = 8
 LOG2E = 1.4426950408889634
 MESH = pl.DeviceIdType.MESH
 
@@ -294,9 +294,10 @@
         launch(j)
     norms()
     forward(0)
+    forward(1)
     for j in range(chunks):
-        if j + 1 < chunks:
-            forward(j + 1)
+        if j + 2 < chunks:
+            forward(j + 2)
         compute(j)
         if j > 0:
             give_back(j - 1)

time: 114 us -> 113 us (level)
  no operation moved by 1% of the time
where the time goes in v5:
time: 113 us
  Pallas kernels  107 us (95%)
  local copies, waits for them, and re-layouts  5.23 us (5%)
  between operations  1.29 us (1%)
    pallas_call x1, Pallas kernels, shards(): pl.pallas_call(functools.partial(kernel, (groups, subs, own, strip, rank,...  107 us
    unnamed x4, local copies, waits for them, and re-layouts  5.23 us

profile of v5, /device:TPU:1, one launch (start us, length us, event | category | flops | bytes accessed | tf_op | source)
XLA Modules:
  0.0 113.3 jit_solution(1618569453236171425)
XLA Ops:
  1.3 106.7 %pair_sketches.1 = (bf16[8,1024,128]{2,1,0:T(8,128)(2,1)}, bf16[32,2,256,128]{3,2,1,0:T(8,128)(2,1)}) custom-call(s32[1]{0:T(128)S(6)} %copy.12.count, s32[1,32]{1,0:T(1,128)} %source_in.1, s32[1,32]{1,0:T(1,128)} %place_in.1, s32[1,32]{1,0:T(1,128)} %partner_in.1, s32[1,32]{1,0:T(1,128)} %ranks_in.1, bf16[32,256,128]{2,1,0:T(8,128)(2,1)} %points.1, ...), custom_call_target="tpu_custom_call" | custom-call | tf_op jit(solution)/shard_map/pair_sketches/pallas_call | solution.py:383
  108.0 0.0 copy-start
  108.0 3.2 %copy.13 = bf16[1,8,1024,128]{3,2,1,0:T(8,128)(2,1)} copy(bf16[1,8,1024,128]{3,2,1,0:T(8,128)(2,1)} %bitcast.7) | data formatting | bytes 4194304
  111.2 0.0 copy-done
  111.2 2.0 %copy.14 = bf16[1,32,2,256,128]{4,3,2,1,0:T(8,128)(2,1)} copy(bf16[1,32,2,256,128]{4,3,2,1,0:T(8,128)(2,1)S(1)} %bitcast.4) | data formatting | bytes 8388608
Async XLA Ops:
  108.0 3.2 %copy-start = (bf16[32,2,256,128]{3,2,1,0:T(8,128)(2,1)S(1)}, bf16[32,2,256,128]{3,2,1,0:T(8,128)(2,1)}, u32[]{:S(2)}) copy-start(bf16[32,2,256,128]{3,2,1,0:T(8,128)(2,1)} %get-tuple-element.5) | copy-start | bytes 12582916
